TPU v7x, 512 devices: a whole 4x8x8 slice. The times are simulated.
512 devices in a mesh: col: 128 (over y, z, core), lev: 4 (over x).
Axes of the slice: x: 4, y: 8, z: 8, core: 2. Of those that a mesh axis runs over, the one named last changes fastest.
Arguments:
- fields: bfloat16 [2, 32, 131072], P(None, 'lev', 'col'), may hold values from 0.5 to 3
- bracket: int32 [8, 131072], P(None, 'col'), may hold values from 0 to 30
- fraction: float32 [8, 131072], P(None, 'col'), may hold values from 0 to 1
- remap_weights: bfloat16 [2048, 128, 128], P('col'), may hold values from 0 to 0.015625
- intersections: int32 [3, 4096], P(None, 'col'), may hold values from 0 to 1023, as said below
- tile_owner: int32 [1024], replicated, may hold values from 0 to 1023, as said below
Outputs:
- normalized: float32 [2, 8, 1024, 128], P(None, 'lev', 'col')
Inputs may be any that keep to these rules, and one draw needn't show every extreme that they name: `intersections`: row 0 names a source block of the entry's own col index; row 1 a target tile whose owner, tile_owner[tile] // 8, lies within 2 indices of the entry's col index or exactly 64 indices away, cyclically; row 2 a weight block of the entry's own col index. `tile_owner`: A permutation of the tiles.
All inputs are finite; a program needn't handle non-finite values.
Results may differ from a plain program's by a relative error of at most 0.00031.
Values may be sent and summed in bfloat16 or wider, within the bound.
No kernel may reach another device: no remote copies, remote signals or barrier semaphores. Data moves between devices by JAX's collectives and lax.ppermute only.
A program may use at most 64 MiB of HBM per device.

v0:
```python
import jax
import jax.numpy as jnp
from jax import lax
from jax.sharding import PartitionSpec as P

F = 2
PLEV = 8
epsilon = 1e-06


def mix_levels(level_block, lower_level, weight_up):
    level_ids = jnp.arange(level_block.shape[1], dtype=jnp.int32)
    is_below = level_ids[None, :, None] == lower_level[:, None, :]
    is_above = level_ids[None, :, None] == lower_level[:, None, :] + 1
    level_coef = jnp.where(
        is_below, 1.0 - weight_up[:, None, :], jnp.where(is_above, weight_up[:, None, :], 0.0)
    )
    return jnp.sum(level_coef[None] * level_block.astype(jnp.float32)[:, None], axis=2)


def gather_rows(selector, partial_tiles):
    return lax.dot_general(
        selector,
        partial_tiles,
        (((0,), (0,)), ((), ())),
        precision=lax.Precision.HIGHEST,
        preferred_element_type=jnp.float32,
    )


def per_device(fields, bracket, fraction, remap_weights, intersections, tile_owner):
    lev_index = lax.axis_index("lev")
    plev_dev = PLEV // lax.axis_size("lev")
    column_levels = lax.all_gather(fields, "lev", axis=1, tiled=True)
    lower_level = lax.dynamic_slice_in_dim(bracket, lev_index * plev_dev, plev_dev, 0)
    weight_up = lax.dynamic_slice_in_dim(fraction, lev_index * plev_dev, plev_dev, 0)
    interp = mix_levels(column_levels, lower_level, weight_up).astype(jnp.bfloat16)
    block_cols = remap_weights.shape[1]
    tile_cells = remap_weights.shape[2]
    blocks = interp.reshape(F, plev_dev, -1, block_cols)
    chosen = jnp.take(blocks, intersections[0], axis=2)
    picked = jnp.take(remap_weights, intersections[2], axis=0)
    partial_tiles = jnp.einsum("fpeb,ebt->efpt", chosen, picked, preferred_element_type=jnp.float32)
    entries = partial_tiles.shape[0]
    partial_tiles = partial_tiles.reshape(entries, -1)
    tile_total = tile_owner.shape[0]
    col_count = lax.axis_size("col")
    tile_dev = tile_total // col_count
    matches = intersections[1][:, None] == jnp.arange(tile_total, dtype=jnp.int32)[None, :]
    slot_index = jnp.sum(jnp.where(matches, tile_owner[None, :], 0), axis=1)
    selector = (
        slot_index[:, None] == jnp.arange(tile_dev * lax.axis_size("col"), dtype=jnp.int32)[None, :]
    ).astype(jnp.float32)
    remapped = lax.psum_scatter(
        gather_rows(selector, partial_tiles), "col", scatter_dimension=0, tiled=True
    )
    remapped = remapped.reshape(tile_dev, F, plev_dev, tile_cells).transpose(1, 2, 0, 3)
    shifted_left = jnp.concatenate([remapped[..., :1], remapped[..., :-1]], axis=-1)
    shifted_right = jnp.concatenate([remapped[..., 1:], remapped[..., -1:]], axis=-1)
    filtered = 0.25 * shifted_left + 0.5 * remapped + 0.25 * shifted_right
    cells = float(tile_dev * tile_cells * col_count)
    local_sums = jnp.sum(filtered, axis=(2, 3))
    field_mean = lax.psum(local_sums, "col") / cells
    centered = filtered - field_mean[:, :, None, None]
    field_var = lax.psum(jnp.sum(centered * centered, axis=(2, 3)), "col") / cells
    return centered * lax.rsqrt(field_var + epsilon)[:, :, None, None]


def solution(mesh):
    in_specs = (
        P(None, "lev", "col"),
        P(None, "col"),
        P(None, "col"),
        P("col", None, None),
        P(None, "col"),
        P(),
    )
    out_specs = P(None, "lev", "col", None)
    return jax.shard_map(
        per_device, mesh=mesh, in_specs=in_specs, out_specs=out_specs, check_vma=False
    )
```

profile of v0, /device:TPU:1, one launch (start us, length us, event | category | flops | bytes accessed | tf_op | source)
XLA Modules:
  0.0 736.7 jit_solution(11726878282647201093)
XLA Ops:
  6.5 0.0 copy-start
  6.5 0.0 reduce-scatter.2.cloned.1.call-start
  6.5 0.7 slice_bitcast_fusion
  7.3 0.8 fusion.11
  8.0 0.8 compare_and_fusion.1
  8.8 0.8 broadcast_add_fusion
  9.6 0.8 broadcast_subtract_fusion
  10.3 10.5 %all_gather.3 = bf16[2,32,1024]{2,1,0:T(8,128)(2,1)S(1)} all-gather(bf16[2,8,1024]{2,1,0:T(8,128)(2,1)} %param.6), channel_id=1, replica_groups=mesh['col'=128,'lev'=4] {'lev'}, dimensions={1}, use_global_device_ids=true | all-gather | bytes 163840 | tf_op jit(solution)/shard_map/all_gather | solution.py:34
  20.9 0.1 multiply_reduce_fusion
  21.0 0.0 copy-start.1
  21.0 0.6 gather_fusion
  21.6 0.0 copy-done
  21.6 0.7 gather_fusion.1
  22.4 0.5 fusion
  22.9 0.1 reshape.97
  22.9 0.0 copy-done.1
  22.9 0.2 select_reduce_fusion
  23.1 2.5 fusion.5
  25.6 0.0 reduce-scatter.2.cloned.1.call-update
  25.6 202.3 %reduce-scatter.2.cloned.1.call-done = f32[8,512]{1,0:T(8,128)} async-done(((f32[1024,512]{1,0:T(8,128)}), f32[8,512]{1,0:T(8,128)}) %reduce-scatter.2.cloned.1.call-update) | async-done | bytes 16400 | tf_op jit(solution)/shard_map/reduce_scatter | solution.py:54
  227.9 0.9 fusion.17
  228.8 0.9 fusion.16
  229.6 0.9 fusion.14
  230.5 251.6 %psum.14 = f32[2,2]{1,0:T(2,128)S(1)} all-reduce(f32[2,2]{1,0:T(2,128)S(1)} %get-tuple-element.5), channel_id=1, replica_groups=mesh['col'=128,'lev'=4] {'col'}, use_global_device_ids=true, to_apply=%region_4.5 | all-reduce | flops 4 | bytes 32 | tf_op jit(solution)/shard_map/psum | solution.py:63
  482.2 0.2 multiply_reduce_fusion.1
  482.3 246.8 %psum.15 = f32[2,2]{1,0:T(2,128)S(1)} all-reduce(f32[2,2]{1,0:T(2,128)S(1)} %multiply_reduce_fusion.1), channel_id=1, replica_groups=mesh['col'=128,'lev'=4] {'col'}, use_global_device_ids=true, to_apply=%region_6.7 | all-reduce | flops 4 | bytes 32 | tf_op jit(solution)/shard_map/psum | solution.py:65
  729.1 0.7 subtract_multiply_fusion
  (5 shorter events, 0.1 us)
Async XLA Ops:
  6.5 15.1 %copy-start = (bf16[16,128,128]{2,1,0:T(8,128)(2,1)S(1)}, bf16[16,128,128]{2,1,0:T(8,128)(2,1)}, u32[]{:S(2)}) copy-start(bf16[16,128,128]{2,1,0:T(8,128)(2,1)} %param.9) | copy-start | bytes 1572868
  6.5 221.4 %reduce-scatter.2.cloned.1.call-start = ((), (), s32[]{:S(2)}) async-start(), calls=%async_computation.1 | async-start | bytes 2113536 | tf_op jit(solution)/shard_map/reduce_scatter | solution.py:54
  21.0 1.9 copy-start.1
Sparse Core Ops, SparseCore 0:
  25.7 202.1 reduce-scatter.1
where the time goes:
time: 737 us
  blocking collectives  509 us (69%)
  waiting for transfers between devices  202 us (27%)
  between operations  13.5 us (2%)
    psum x1, blocking collectives, per_device(): field_mean = lax.psum(local_sums, 'col') / cells  252 us
    psum x1, blocking collectives, per_device(): lax.psum(jnp.sum(centered * centered, axis=(2, 3)), 'col') / cells  247 us
    reduce_scatter x1, waiting for transfers between devices, per_device(): lax.psum_scatter(gather_rows(selector, partial_tiles), 'col', scatter_dim...  202 us
  transfers between devices with their start and end apart: 1, of which 1 were waited for; matrix products, arithmetic and copies ran while one was open for 0% of the time, Pallas kernels for 0%

commit v1 on v0

--- a/solution.py
+++ b/solution.py
@@ -60,7 +60,7 @@
     filtered = 0.25 * shifted_left + 0.5 * remapped + 0.25 * shifted_right
     cells = float(tile_dev * tile_cells * col_count)
     local_sums = jnp.sum(filtered, axis=(2, 3))
-    field_mean = lax.psum(local_sums, "col") / cells
+    field_mean = jnp.sum(lax.all_gather(local_sums, "col"), axis=0) / cells
     centered = filtered - field_mean[:, :, None, None]
     field_var = lax.psum(jnp.sum(centered * centered, axis=(2, 3)), "col") / cells
     return centered * lax.rsqrt(field_var + epsilon)[:, :, None, None]

time: 737 us -> 541 us (0.73)
  blocking collectives: 509 us -> 311 us
    psum x1 -> x0, blocking collectives: 252 us -> none  [per_device(): field_mean = lax.psum(local_sums, 'col') / cells]
    all_gather x0 -> x1, blocking collectives: none -> 53.9 us  [per_device(): field_mean = jnp.sum(lax.all_gather(local_sums, 'col'), axis=0) / cells]
where the time goes in v1:
time: 541 us; the launch traced here: 539 us
  blocking collectives  311 us (57%)
  waiting for transfers between devices  202 us (37%)
  between operations  13.5 us (2%)
    psum x1, blocking collectives, per_device(): lax.psum(jnp.sum(centered * centered, axis=(2, 3)), 'col') / cells  246 us
    reduce_scatter x1, waiting for transfers between devices, per_device(): lax.psum_scatter(gather_rows(selector, partial_tiles), 'col', scatter_dim...  202 us
    all_gather x1, blocking collectives, per_device(): field_mean = jnp.sum(lax.all_gather(local_sums, 'col'), axis=0) / cells  53.9 us
  transfers between devices with their start and end apart: 1, of which 1 were waited for; matrix products, arithmetic and copies ran while one was open for 0% of the time, Pallas kernels for 0%

profile of v1, /device:TPU:1, one launch (start us, length us, event | category | flops | bytes accessed | tf_op | source)
XLA Modules:
  0.0 538.6 jit_solution(3085503436206874832)
XLA Ops:
  6.5 0.0 copy-start
  6.5 0.0 reduce-scatter.2.cloned.1.call-start
  6.5 0.7 slice_bitcast_fusion
  7.3 0.8 fusion.11
  8.0 0.8 compare_and_fusion.1
  8.8 0.8 broadcast_add_fusion
  9.6 0.8 broadcast_subtract_fusion
  10.3 10.5 %all_gather.9 = bf16[2,32,1024]{2,1,0:T(8,128)(2,1)S(1)} all-gather(bf16[2,8,1024]{2,1,0:T(8,128)(2,1)} %param.6), channel_id=1, replica_groups=mesh['col'=128,'lev'=4] {'lev'}, dimensions={1}, use_global_device_ids=true | all-gather | bytes 163840 | tf_op jit(solution)/shard_map/all_gather | solution.py:34
  20.9 0.1 multiply_reduce_fusion
  21.0 0.0 copy-start.1
  21.0 0.6 gather_fusion
  21.6 0.0 copy-done
  21.6 0.7 gather_fusion.1
  22.4 0.5 fusion
  22.9 0.1 reshape.99
  22.9 0.0 copy-done.1
  22.9 0.2 select_reduce_fusion
  23.1 2.5 fusion.5
  25.6 0.0 reduce-scatter.2.cloned.1.call-update
  25.6 202.3 %reduce-scatter.2.cloned.1.call-done = f32[8,512]{1,0:T(8,128)} async-done(((f32[1024,512]{1,0:T(8,128)}), f32[8,512]{1,0:T(8,128)}) %reduce-scatter.2.cloned.1.call-update) | async-done | bytes 16400 | tf_op jit(solution)/shard_map/reduce_scatter | solution.py:54
  227.9 0.9 fusion.17
  228.8 0.9 fusion.16
  229.6 0.9 fusion.14
  230.5 53.9 %all-gather.1 = f32[128,2,2]{2,1,0:T(2,128)S(1)} all-gather(f32[1,2,2]{2,1,0:T(2,128)S(1)} %bitcast.34), channel_id=2, replica_groups=mesh['col'=128,'lev'=4] {'col'}, dimensions={0}, use_global_device_ids=true | all-gather | bytes 2064 | tf_op jit(solution)/shard_map/all_gather | solution.py:63
  284.4 0.1 reduce_sum.48
  284.6 0.2 multiply_reduce_fusion.1
  284.7 246.3 %psum.7 = f32[2,2]{1,0:T(2,128)S(1)} all-reduce(f32[2,2]{1,0:T(2,128)S(1)} %multiply_reduce_fusion.1), channel_id=1, replica_groups=mesh['col'=128,'lev'=4] {'col'}, use_global_device_ids=true, to_apply=%region_6.7 | all-reduce | flops 4 | bytes 32 | tf_op jit(solution)/shard_map/psum | solution.py:65
  531.1 0.7 subtract_multiply_fusion
  (5 shorter events, 0.1 us)
Async XLA Ops:
  6.5 15.1 %copy-start = (bf16[16,128,128]{2,1,0:T(8,128)(2,1)S(1)}, bf16[16,128,128]{2,1,0:T(8,128)(2,1)}, u32[]{:S(2)}) copy-start(bf16[16,128,128]{2,1,0:T(8,128)(2,1)} %param.9) | copy-start | bytes 1572868
  6.5 221.4 %reduce-scatter.2.cloned.1.call-start = ((), (), s32[]{:S(2)}) async-start(), calls=%async_computation.1 | async-start | bytes 2113536 | tf_op jit(solution)/shard_map/reduce_scatter | solution.py:54
  21.0 1.9 copy-start.1
Sparse Core Ops, SparseCore 0:
  25.7 202.1 reduce-scatter.1
